TPU v7x, 32 devices: a whole 2x2x4 slice. The times are simulated.
32 devices in a mesh: dp: 8 (over y, x, core), tensor: 4 (over z).
Axes of the slice: x: 2, y: 2, z: 4, core: 2. Of those that a mesh axis runs over, the one named last changes fastest.
Arguments:
- tokens: bfloat16 [4096, 2048], P('dp'), may hold values from -6 to 6
- seq_ids: int32 [4096], replicated, may hold values from 0 to 3, never falling along the last dimension, each value on 1 to 2048 neighbouring positions
- route_ids: int32 [4096, 6], P('dp'), may hold values from 0 to 63, all different within a row; in each aligned block of 512 rows (0 to 511, 512 to 1023, ...) at most 72 rows name the same one
- cotangent: bfloat16 [4096, 2048], P('dp'), may hold values from -6 to 6
- input_gain: float32 [2048], replicated, may hold values from 0.5 to 1.5
- w_query: bfloat16 [2048, 3072], P(None, 'tensor'), may hold values from -0.125 to 0.125
- w_latent: bfloat16 [2048, 576], replicated, may hold values from -0.125 to 0.125
- latent_gain: float32 [512], replicated, may hold values from 0.5 to 1.5
- w_expand: bfloat16 [512, 4096], P(None, 'tensor'), may hold values from -0.25 to 0.25
- w_out: bfloat16 [2048, 2048], P('tensor'), may hold values from -0.5 to 0.5
- middle_gain: float32 [2048], replicated, may hold values from 0.5 to 1.5
- w_router: bfloat16 [2048, 64], replicated, may hold values from -0.0390625 to 0.0390625
- expert_gate: bfloat16 [64, 2048, 1408], P('dp', None, 'tensor'), may hold values from -0.125 to 0.125
- expert_up: bfloat16 [64, 2048, 1408], P('dp', None, 'tensor'), may hold values from -0.125 to 0.125
- expert_down: bfloat16 [64, 1408, 2048], P('dp', 'tensor'), may hold values from -2.5 to 2.5
- shared_gate: bfloat16 [2048, 2816], P(None, 'tensor'), may hold values from -0.125 to 0.125
- shared_up: bfloat16 [2048, 2816], P(None, 'tensor'), may hold values from -0.125 to 0.125
- shared_down: bfloat16 [2816, 2048], P('tensor'), may hold values from -0.21875 to 0.21875
Outputs:
- output: bfloat16 [4096, 2048], P('dp')
- token_grad: bfloat16 [4096, 2048], P('dp')
- grad_input_gain: float32 [2048], P('dp')
- grad_query: float32 [2048, 3072], P('dp', 'tensor')
- grad_latent: float32 [2048, 576], P('dp')
- grad_latent_gain: float32 [512], P('dp')
- grad_expand: float32 [512, 4096], P('dp', 'tensor')
- grad_out_proj: float32 [2048, 2048], P('tensor', 'dp')
- grad_middle_gain: float32 [2048], P('dp')
- grad_router: float32 [2048, 64], P('dp')
- grad_expert_gate: float32 [64, 2048, 1408], P('dp', None, 'tensor')
- grad_expert_up: float32 [64, 2048, 1408], P('dp', None, 'tensor')
- grad_expert_down: float32 [64, 1408, 2048], P('dp', 'tensor')
- grad_shared_gate: float32 [2048, 2816], P('dp', 'tensor')
- grad_shared_up: float32 [2048, 2816], P('dp', 'tensor')
- grad_shared_down: float32 [2816, 2048], P('tensor', 'dp')
Inputs may be any that keep to these rules, and one draw needn't show every extreme that they name: seq_ids never fall; each sequence has 1 to 2048 tokens, one has exactly 2048. `route_ids`: each row names 6 different experts; in the rows of one data block (512 tokens) no expert is named by more than 72 rows, a bound that some block reaches.
All inputs are finite; a program needn't handle non-finite values.
Results may differ from a plain program's by a relative error of at most 0.025.
Values may be sent and summed in bfloat16 or wider, within the bound.
No kernel may reach another device: no remote copies, remote signals or barrier semaphores. Data moves between devices by JAX's collectives and lax.ppermute only.
A program may use at most 448 MiB of HBM per device.

v0:
```python
import jax
import jax.numpy as jnp
from jax import lax
from jax.sharding import PartitionSpec as P

DN = 128
DR = 64
DV = 128
KVR = 512
REACH = 4
CAP = 72
BF = jnp.bfloat16
F32 = jnp.float32
epsilon = 1e-06


def dot(eq, a, b):
    return jnp.einsum(eq, a, b, preferred_element_type=F32)


def passed_along(shard, axis, by):
    peers = lax.axis_size(axis)
    pairs = [(i, i + by) for i in range(peers) if 0 <= i + by < peers]
    return lax.ppermute(shard, axis, pairs)


def normed(values, norm_gain):
    return (
        values * lax.rsqrt(jnp.mean(values * values, axis=-1, keepdims=True) + epsilon) * norm_gain
    )


def norm_backward(values, norm_gain, upstream):
    _, pullback = jax.vjp(normed, values, norm_gain)
    return pullback(upstream)


def rotate(values, cosine, sine):
    half = values.shape[-1] // 2
    front, back = (values[..., :half], values[..., half:])
    return jnp.concatenate([front * cosine - back * sine, back * cosine + front * sine], axis=-1)


def rotate_back(upstream, cosine, sine):
    return rotate(upstream, cosine, -sine)


def silu_gate(gate_val, up_val):
    return gate_val * jax.nn.sigmoid(gate_val) * up_val


def silu_backward(gate_val, up_val, upstream):
    _, pullback = jax.vjp(silu_gate, gate_val, up_val)
    return pullback(upstream)


def rope_tables(seq_all, seq_here, index_here):
    starts = jnp.sum((seq_all[None, :] < seq_here[:, None]).astype(jnp.int32), axis=1)
    position = (index_here - starts).astype(F32)
    frequency = 10000.0 ** (-(jnp.arange(DR // 2, dtype=F32) * 2.0) / DR)
    angle = position[:, None] * frequency[None, :]
    return (jnp.cos(angle), jnp.sin(angle))


def scatter_sum(parts):
    joined = jnp.concatenate(parts, axis=1)
    summed = lax.psum_scatter(joined, "dp", scatter_dimension=0, tiled=True)
    out, at = ([], 0)
    for part in parts:
        out.append(summed[:, at : at + part.shape[1]].astype(F32))
        at += part.shape[1]
    return out


def shards(
    tokens,
    seq_ids,
    route_ids,
    cotangent,
    input_gain,
    w_query,
    w_latent,
    latent_gain,
    w_expand,
    w_out,
    middle_gain,
    w_router,
    expert_gate,
    expert_up,
    expert_down,
    shared_gate,
    shared_up,
    shared_down,
):
    devices = lax.axis_size("dp")
    rank_dp = lax.axis_index("dp")
    tok_rows, width = tokens.shape
    experts_local = expert_gate.shape[0]
    heads_local = w_query.shape[1] // (DN + DR)
    reach = min(REACH, devices - 1)
    window = (reach + 1) * tok_rows
    scale = (DN + DR) ** (-0.5)
    cot_all = lax.all_gather(cotangent, "dp", tiled=True)
    route_all = lax.all_gather(route_ids, "dp", tiled=True)
    index_here = rank_dp * tok_rows + jnp.arange(tok_rows, dtype=jnp.int32)
    seq_here = lax.dynamic_slice_in_dim(seq_ids, rank_dp * tok_rows, tok_rows, 0)
    cosine, sine = rope_tables(seq_ids, seq_here, index_here)
    key_index = (rank_dp - reach) * tok_rows + jnp.arange(window, dtype=jnp.int32)
    seq_padded = jnp.concatenate([jnp.full((reach * tok_rows,), -1, jnp.int32), seq_ids])
    seq_keys = lax.dynamic_slice_in_dim(seq_padded, rank_dp * tok_rows, window, 0)
    allowed = (seq_here[:, None] == seq_keys[None, :]) & (key_index[None, :] <= index_here[:, None])
    token_features = tokens.astype(F32)
    grad_output = cotangent.astype(F32)
    hidden_in = normed(token_features, input_gain).astype(BF)
    latent_full = jnp.dot(hidden_in, w_latent, preferred_element_type=F32)
    latent_raw = latent_full[:, :KVR]
    latent = normed(latent_raw, latent_gain).astype(BF)
    rope_key = rotate(latent_full[:, KVR:], cosine, sine).astype(BF)
    own_keys = jnp.concatenate([latent, rope_key], axis=1)
    earlier = [passed_along(own_keys, "dp", back) for back in range(reach, 0, -1)]
    keys_window = jnp.concatenate(earlier + [own_keys], axis=0)
    latent_window = keys_window[:, :KVR]
    rope_window = keys_window[:, KVR:]
    query_pre = jnp.dot(hidden_in, w_query, preferred_element_type=F32).reshape(
        tok_rows, heads_local, DN + DR
    )
    queries = jnp.concatenate(
        [query_pre[..., :DN], rotate(query_pre[..., DN:], cosine[:, None, :], sine[:, None, :])],
        axis=-1,
    ).astype(BF)
    expanded = (
        jnp.dot(latent_window, w_expand, preferred_element_type=F32)
        .astype(BF)
        .reshape(window, heads_local, DN + DV)
    )
    key_nope = expanded[..., :DN]
    key_value = expanded[..., DN:]
    scores = dot("qhd,khd->hqk", queries[..., :DN], key_nope) + dot(
        "qhd,kd->hqk", queries[..., DN:], rope_window
    )
    scores = jnp.where(allowed[None], scores * scale, -1e30)
    probs = jax.nn.softmax(scores, axis=-1)
    probs_low = probs.astype(BF)
    attended = (
        dot("hqk,khd->qhd", probs_low, key_value).astype(BF).reshape(tok_rows, heads_local * DV)
    )
    attention = lax.psum(
        jnp.dot(attended, w_out, preferred_element_type=F32).astype(BF), "tensor"
    ).astype(F32)
    middle = token_features + attention
    hidden_mid = normed(middle, middle_gain).astype(BF)
    hidden_all = lax.all_gather(hidden_mid, "dp", tiled=True)
    shared_gate_val = jnp.dot(hidden_mid, shared_gate, preferred_element_type=F32)
    shared_up_val = jnp.dot(hidden_mid, shared_up, preferred_element_type=F32)
    shared_active = silu_gate(shared_gate_val, shared_up_val).astype(BF)
    shared_result = jnp.dot(shared_active, shared_down, preferred_element_type=F32)
    shared_active_grad = dot("td,fd->tf", cotangent, shared_down)
    shared_gate_grad, shared_up_grad = silu_backward(
        shared_gate_val, shared_up_val, shared_active_grad
    )
    shared_gate_grad = shared_gate_grad.astype(BF)
    shared_up_grad = shared_up_grad.astype(BF)
    mid_from_shared = dot("tf,df->td", shared_gate_grad, shared_gate) + dot(
        "tf,df->td", shared_up_grad, shared_up
    )
    grad_shared_down = dot("td,tf->df", cotangent, shared_active).astype(BF)
    grad_shared_gate = dot("td,tf->df", hidden_mid, shared_gate_grad).astype(BF)
    grad_shared_up = dot("td,tf->df", hidden_mid, shared_up_grad).astype(BF)
    local_ids = rank_dp * experts_local + jnp.arange(experts_local, dtype=jnp.int32)
    named = jnp.any(route_all[:, :, None] == local_ids[None, None, :], axis=1)
    named_block = named.reshape(devices, tok_rows, experts_local)
    before = jnp.tril(jnp.ones((tok_rows, tok_rows), BF), -1)
    rank_within = dot("ts,bse->bet", before, named_block.astype(BF)).astype(jnp.int32)
    slot = jnp.where(named_block.transpose(0, 2, 1), rank_within, -1)
    chosen = (slot[:, :, None, :] == jnp.arange(CAP, dtype=jnp.int32)[None, None, :, None]).astype(
        BF
    )
    logits = jnp.dot(hidden_all, w_router, preferred_element_type=F32)
    router_probs = jax.nn.softmax(logits, axis=-1)
    local_probs = lax.dynamic_slice_in_dim(
        router_probs, rank_dp * experts_local, experts_local, 1
    ).reshape(devices, tok_rows, experts_local)
    slot_gates = jnp.sum(
        chosen.astype(F32) * local_probs.transpose(0, 2, 1)[:, :, None, :], axis=-1
    )
    cot_rows = dot("bect,btd->becd", chosen, cot_all.reshape(devices, tok_rows, width)).astype(BF)
    rows = dot("bect,btd->becd", chosen, hidden_all.reshape(devices, tok_rows, width)).astype(BF)
    gate_val = dot("becd,edf->becf", rows, expert_gate)
    up_val = dot("becd,edf->becf", rows, expert_up)
    down_back = dot("becd,efd->becf", cot_rows, expert_down)
    active = silu_gate(gate_val, up_val).astype(BF)
    gated_active = active.astype(F32) * slot_gates[..., None]
    gate_grad = jnp.sum(active.astype(F32) * down_back, axis=-1)
    gate_val_grad, up_val_grad = silu_backward(gate_val, up_val, down_back * slot_gates[..., None])
    gate_val_grad = gate_val_grad.astype(BF)
    up_val_grad = up_val_grad.astype(BF)
    gated_active = gated_active.astype(BF)
    row_grad = (
        dot("becf,edf->becd", gate_val_grad, expert_gate)
        + dot("becf,edf->becd", up_val_grad, expert_up)
    ).astype(BF)
    row_out = dot("becf,efd->becd", gated_active, expert_down).astype(BF)
    probs_grad = dot("bect,bec->bte", chosen, gate_grad.astype(BF)).reshape(-1, experts_local)
    probs_grad = lax.dynamic_update_slice_in_dim(
        jnp.zeros_like(router_probs), probs_grad, rank_dp * experts_local, 1
    )
    logit_grad = (
        router_probs * (probs_grad - jnp.sum(router_probs * probs_grad, axis=-1, keepdims=True))
    ).astype(BF)
    grad_router = dot("td,te->de", hidden_all, logit_grad)
    mid_part = dot("bect,becd->btd", chosen, row_grad).reshape(-1, width) + dot(
        "te,de->td", logit_grad, w_router
    )
    mid_block = lax.psum_scatter(mid_part.astype(BF), "dp", scatter_dimension=0, tiled=True)
    mid_grad = lax.psum((mid_block.astype(F32) + mid_from_shared).astype(BF), "tensor").astype(F32)
    routed_part = dot("bect,becd->btd", chosen, row_out).reshape(-1, width).astype(BF)
    routed_part, _ = lax.optimization_barrier((routed_part, mid_block))
    routed_block = lax.psum_scatter(routed_part, "dp", scatter_dimension=0, tiled=True)
    grad_expert_down = dot("becf,becd->efd", gated_active, cot_rows)
    grad_expert_gate = dot("becd,becf->edf", rows, gate_val_grad)
    grad_expert_up = dot("becd,becf->edf", rows, up_val_grad)
    middle_from_norm, grad_middle_gain = norm_backward(middle, middle_gain, mid_grad)
    middle_grad = grad_output + middle_from_norm
    middle_low = middle_grad.astype(BF)
    grad_out_proj = dot("td,tc->dc", middle_low, attended).astype(BF)
    attended_grad = (
        dot("td,cd->tc", middle_low, w_out).astype(BF).reshape(tok_rows, heads_local, DV)
    )
    probs_grad_att = dot("qhd,khd->hqk", attended_grad, key_value)
    score_grad = (
        probs * (probs_grad_att - jnp.sum(probs * probs_grad_att, axis=-1, keepdims=True))
    ).astype(BF)
    query_nope_grad = dot("hqk,khd->qhd", score_grad, key_nope) * scale
    query_rope_grad = dot("hqk,kd->qhd", score_grad, rope_window) * scale
    key_nope_grad = dot("hqk,qhd->khd", score_grad, queries[..., :DN]) * scale
    rope_window_grad = dot("hqk,qhd->kd", score_grad, queries[..., DN:]) * scale
    value_grad = dot("hqk,qhd->khd", probs_low, attended_grad)
    expanded_grad = (
        jnp.concatenate([key_nope_grad, value_grad], axis=-1)
        .astype(BF)
        .reshape(window, heads_local * (DN + DV))
    )
    latent_window_grad = dot("wc,kc->wk", expanded_grad, w_expand)
    grad_expand = dot("wk,wc->kc", latent_window, expanded_grad).astype(BF)
    window_grad = jnp.concatenate([latent_window_grad, rope_window_grad], axis=1)
    keys_grad = window_grad[reach * tok_rows :]
    for back in range(reach, 0, -1):
        start = (reach - back) * tok_rows
        piece = window_grad[start : start + tok_rows].astype(BF)
        keys_grad = keys_grad + passed_along(piece, "dp", -back).astype(F32)
    query_grad = (
        jnp.concatenate(
            [query_nope_grad, rotate_back(query_rope_grad, cosine[:, None, :], sine[:, None, :])],
            axis=-1,
        )
        .astype(BF)
        .reshape(tok_rows, heads_local * (DN + DR))
    )
    grad_query = dot("td,tc->dc", hidden_in, query_grad).astype(BF)
    input_from_query = dot("tc,dc->td", query_grad, w_query)
    keys_grad = lax.psum(keys_grad.astype(BF), "tensor").astype(F32)
    latent_raw_grad, grad_latent_gain = norm_backward(latent_raw, latent_gain, keys_grad[:, :KVR])
    rope_raw_grad = rotate_back(keys_grad[:, KVR:], cosine, sine)
    latent_full_grad = jnp.concatenate([latent_raw_grad, rope_raw_grad], axis=-1).astype(BF)
    grad_latent = dot("td,tc->dc", hidden_in, latent_full_grad).astype(BF)
    input_grad = lax.psum(input_from_query.astype(BF), "tensor").astype(F32) + dot(
        "tc,dc->td", latent_full_grad, w_latent
    )
    token_from_norm, grad_input_gain = norm_backward(token_features, input_gain, input_grad)
    token_grad = (middle_grad + token_from_norm).astype(BF)
    routed_block, _ = lax.optimization_barrier((routed_block, mid_grad))
    feedforward = lax.psum((routed_block.astype(F32) + shared_result).astype(BF), "tensor")
    output = (middle + feedforward.astype(F32)).astype(BF)
    grad_shared_down, grad_shared_gate, grad_shared_up = scatter_sum(
        [grad_shared_down, grad_shared_gate, grad_shared_up]
    )
    grad_router = lax.psum(grad_router.astype(BF), "tensor")
    gains = jnp.stack(
        [grad_middle_gain, grad_input_gain, jnp.repeat(grad_latent_gain, width // KVR)], axis=1
    ).astype(BF)
    grad_out_proj, grad_query, grad_latent, grad_expand, grad_router, gains = scatter_sum(
        [grad_out_proj, grad_query, grad_latent, grad_expand.reshape(width, -1), grad_router, gains]
    )
    grad_expand = grad_expand.reshape(KVR // devices, -1)
    return (
        output,
        token_grad,
        gains[:, 1],
        grad_query,
        grad_latent,
        gains[:: width // KVR, 2],
        grad_expand,
        grad_out_proj.T,
        gains[:, 0],
        grad_router,
        grad_expert_gate,
        grad_expert_up,
        grad_expert_down,
        grad_shared_gate,
        grad_shared_up,
        grad_shared_down.T,
    )


def solution(mesh):
    placed = (
        P("dp", None),
        P(),
        P("dp", None),
        P("dp", None),
        P(),
        P(None, "tensor"),
        P(),
        P(),
        P(None, "tensor"),
        P("tensor", None),
        P(),
        P(),
        P("dp", None, "tensor"),
        P("dp", None, "tensor"),
        P("dp", "tensor", None),
        P(None, "tensor"),
        P(None, "tensor"),
        P("tensor", None),
    )
    return jax.shard_map(
        shards,
        mesh=mesh,
        in_specs=placed,
        out_specs=(
            P("dp", None),
            P("dp", None),
            P("dp"),
            P("dp", "tensor"),
            P("dp", None),
            P("dp"),
            P("dp", "tensor"),
            P("tensor", "dp"),
            P("dp"),
            P("dp", None),
            P("dp", None, "tensor"),
            P("dp", None, "tensor"),
            P("dp", "tensor", None),
            P("dp", "tensor"),
            P("dp", "tensor"),
            P("tensor", "dp"),
        ),
        check_vma=False,
    )
```

profile of v0, /device:TPU:0, one launch (start us, length us, event | category | flops | bytes accessed | tf_op | source)
XLA Modules:
  0.0 1195.1 jit_solution(14079437632044810351)
XLA Ops:
  13.4 3.8 fusion.161
  20.9 5.7 collective-permute-start
  26.6 3.4 collective-permute-start.1
  29.9 3.0 collective-permute-start.2
  36.3 3.5 fusion.159
  40.0 25.1 %collective-permute-done = bf16[512,576]{0,1:T(8,128)(2,1)} collective-permute-done((bf16[512,576]{0,1:T(8,128)(2,1)}, bf16[512,576]{0,1:T(8,128)(2,1)}, u32[]{:S(2)}, u32[]{:S(2)}) %collective-permute-start) | collective-permute-done | bytes 589856 | tf_op jit(solution)/shard_map/ppermute | solution.py:24
  69.6 3.4 convolution_convert_fusion.2
  73.0 8.9 fusion.82
  82.0 13.6 %fusion.3 = f32[4,512,2560]{2,1,0:T(8,128)} fusion(f32[4,512,2560]{2,1,0:T(8,128)} %fusion.82, pred[512,2560]{1,0:T(8,128)(4,1)S(1)} %compare_and_fusion, bf16[2560,576]{0,1:T(8,128)(2,1)} %copy-done.37, bf16[512,4,32]{0,2,1:T(8,128)(2,1)S(1)} %get-tuple-element.126, bf16[512,4,32]{0,2,1:T(8,128)(2,1)S(1)} %get-tuple-element.125), kind=kOutput, calls=%fused_computation.7 | convolution fusion | flops 687341568 | bytes 43843584 | tf_op jit(solution)/shard_map/qhd,kd->hqk/dot_general | solution.py:18
  95.6 23.5 %fusion.169 = (f32[4,512]{1,0:T(4,128)S(1)}, f32[4,512,2560]{2,1,0:T(8,128)}) fusion(f32[4,512,2560]{2,1,0:T(8,128)} %fusion.3), kind=kOutput, calls=%fused_computation.251 | output fusion | flops 10488319 | bytes 41951232 | tf_op jit(solution)/shard_map/sub | solution.py:142
  119.1 17.4 %fusion.105 = bf16[4,128,512]{2,1,0:T(8,128)(2,1)} fusion(bf16[2560,4,256]{0,2,1:T(8,128)(2,1)} %bitcast.238, f32[4,512]{1,0:T(4,128)S(1)} %get-tuple-element.144, f32[4,512,2560]{2,1,0:T(8,128)} %fusion.3), kind=kOutput, calls=%fused_computation.147 | convolution fusion | flops 1358172672 | bytes 45096960 | tf_op jit(solution)/shard_map/hqk,khd->qhd/dot_general | solution.py:18
  136.5 4.4 convolution_convert_fusion.10
  141.5 91.4 %all-reduce.6.cloned.1.call-done = bf16[512,2048]{1,0:T(8,128)(2,1)} async-done(((bf16[512,2048]{1,0:T(8,128)(2,1)}), bf16[512,2048]{1,0:T(8,128)(2,1)}) %all-reduce.6.cloned.1.call-update) | async-done | bytes 2097168 | tf_op jit(solution)/shard_map/psum | solution.py:147
  232.9 3.1 multiply_reduce_fusion.4
  239.6 9.4 all_gather.9
  249.6 3.0 iota_compare_fusion.14
  252.7 18.8 %convolution_convert_fusion = bf16[8,8,72,2048]{3,2,1,0:T(8,128)(2,1)} fusion(bf16[8,512,2048,1]{2,1,3,0:T(8,128)(2,1)} %bitcast.249, s32[8,8,512]{2,1,0:T(8,128)S(1)} %fusion.120), kind=kOutput, calls=%fused_computation.26 | convolution fusion | flops 9675472896 | bytes 35782656 | tf_op jit(solution)/shard_map/bect,btd->becd/dot_general | solution.py:18
  271.4 59.2 %all-gather.3.cloned.1.call-done = bf16[4096,2048]{1,0:T(8,128)(2,1)} async-done(((bf16[512,2048]{1,0:T(8,128)(2,1)}), bf16[4096,2048]{1,0:T(8,128)(2,1)}) %all-gather.3.cloned.1.call-update) | async-done | bytes 16777232 | tf_op jit(solution)/shard_map/all_gather | solution.py:152
  330.6 18.8 %convolution_convert_fusion.1 = bf16[8,8,72,2048]{3,2,1,0:T(8,128)(2,1)} fusion(bf16[8,512,2048,1]{2,1,3,0:T(8,128)(2,1)} %bitcast.222, s32[8,8,512]{2,1,0:T(8,128)S(1)} %fusion.120), kind=kOutput, calls=%fused_computation.27 | convolution fusion | flops 9675472896 | bytes 35782656 | tf_op jit(solution)/shard_map/bect,btd->becd/dot_general | solution.py:18
  349.4 20.0 %fusion.18 = f32[8,8,72,352]{3,2,1,0:T(8,128)} fusion(bf16[8,8,72,2048]{3,2,1,0:T(8,128)(2,1)} %convolution_convert_fusion.1, bf16[8,2048,352]{1,2,0:T(8,128)(2,1)} %param.31), kind=kOutput, calls=%fused_computation.22 | convolution fusion | flops 6643777536 | bytes 36896768 | tf_op jit(solution)/shard_map/becd,edf->becf/dot_general | solution.py:18
  369.4 20.4 %fusion.20 = f32[8,8,72,352]{3,2,1,0:T(8,128)} fusion(bf16[8,8,72,2048]{3,2,1,0:T(8,128)(2,1)} %convolution_convert_fusion.1, bf16[8,2048,352]{1,2,0:T(8,128)(2,1)} %param.30), kind=kOutput, calls=%fused_computation.24 | convolution fusion | flops 6643777536 | bytes 36896768 | tf_op jit(solution)/shard_map/becd,edf->becf/dot_general | solution.py:18
  389.9 24.2 %fusion.39 = (bf16[8,8,72]{2,0,1:T(8,128)(2,1)S(1)}, bf16[8,8,72,352]{3,2,0,1:T(8,128)(2,1)}, f32[8,8,72,352]{3,2,1,0:T(8,128)}) fusion(f32[8,8,72,352]{3,2,1,0:T(8,128)} %fusion.18, f32[8,8,72,352]{3,2,1,0:T(8,128)} %fusion.20, bf16[8,352,2048]{2,1,0:T(8,128)(2,1)} %param.32, bf16[8,8,72,2048]{3,2,1,0:T(8,128)(2,1)} %convolution_convert_fusion), kind=kOutput, calls=%fused_computation.56 | convolution fusion | flops 6658371072 | bytes 53126144 | tf_op jit(solution)/shard_map/becd,efd->becf/dot_general | solution.py:18
  415.7 11.1 fusion.170
  429.9 6.7 multiply_convert_fusion.1
  436.6 21.0 %fusion.31 = f32[8,8,72,2048]{3,2,0,1:T(8,128)} fusion(bf16[8,2048,352]{1,2,0:T(8,128)(2,1)} %param.30, bf16[8,8,72,352]{3,2,0,1:T(8,128)(2,1)} %get-tuple-element.115), kind=kOutput, calls=%fused_computation.33 | convolution fusion | flops 6643777536 | bytes 52527104 | tf_op jit(solution)/shard_map/becf,edf->becd/dot_general | solution.py:18
  457.6 40.2 %fusion.5 = f32[8,512,2048,1]{2,1,3,0:T(8,128)} fusion(f32[8,8,72,2048]{3,2,0,1:T(8,128)} %fusion.31, bf16[8,2048,352]{1,2,0:T(8,128)(2,1)} %param.31, bf16[8,8,72,352]{3,2,0,1:T(8,128)(2,1)} %get-tuple-element.114, pred[8,8,72,512]{3,2,1,0:T(8,128)(4,1)} %iota_compare_fusion.14), kind=kOutput, calls=%fused_computation.12 | convolution fusion | flops 16326328320 | bytes 88440832 | tf_op jit(solution)/shard_map/bect,becd->btd/dot_general | solution.py:18
  497.8 17.1 %fusion.1 = bf16[4096,2048]{1,0:T(8,128)(2,1)} fusion(f32[8,512,2048,1]{2,1,3,0:T(8,128)} %fusion.5, bf16[4096,64]{0,1:T(8,128)(2,1)} %multiply_convert_fusion.6, bf16[2048,64]{0,1:T(8,128)(2,1)S(1)} %copy-done.31), kind=kOutput, calls=%fused_computation.3 | convolution fusion | flops 1090519040 | bytes 51118080 | tf_op jit(solution)/shard_map/te,de->td/dot_general | solution.py:18
  515.4 3.0 iota_compare_fusion.13
  518.3 4.8 fusion.171
  526.6 3.3 multiply_convert_fusion.5
  530.8 4.1 fusion.173
  534.9 95.9 %reduce-scatter.5.cloned.1.call-done = bf16[512,2048]{1,0:T(8,128)(2,1)} async-done(((bf16[4096,2048]{1,0:T(8,128)(2,1)}), bf16[512,2048]{1,0:T(8,128)(2,1)}) %reduce-scatter.5.cloned.1.call-update) | async-done | bytes 2097168 | tf_op jit(solution)/shard_map/reduce_scatter | solution.py:214
  630.9 7.1 add_convert_fusion.3
  638.2 29.4 %bitcast_convert_fusion = bf16[8,512,2048]{2,1,0:T(8,128)(2,1)} fusion(bf16[8,352,2048]{2,1,0:T(8,128)(2,1)} %param.32, bf16[8,8,72,352]{3,2,0,1:T(8,128)(2,1)} %get-tuple-element.136, pred[8,8,72,512]{3,2,1,0:T(8,128)(4,1)} %iota_compare_fusion.13), kind=kOutput, calls=%fused_computation.4 | convolution fusion | flops 16325279744 | bytes 33914880 | tf_op jit(solution)/shard_map/bect,becd->btd/dot_general | solution.py:18
  667.7 10.2 convolution_convert_fusion.11
  677.9 46.8 %all-reduce.8.cloned.1.call-done = bf16[512,2048]{1,0:T(8,128)(2,1)} async-done(((bf16[512,2048]{1,0:T(8,128)(2,1)}), bf16[512,2048]{1,0:T(8,128)(2,1)}) %all-reduce.8.cloned.1.call-update) | async-done | bytes 2097168 | tf_op jit(solution)/shard_map/psum | solution.py:215
  724.7 4.9 multiply_reduce_fusion.2
  729.7 5.4 convolution_convert_fusion.12
  735.0 19.7 %fusion.69 = bf16[2560,4,128]{0,2,1:T(8,128)(2,1)} fusion(bf16[512,4,128]{0,2,1:T(8,128)(2,1)} %bitcast.252, f32[4,512]{1,0:T(4,128)S(1)} %copy-done.48, f32[4,512,2560]{2,1,0:T(8,128)} %fusion.3), kind=kOutput, calls=%fused_computation.106 | convolution fusion | flops 1359221248 | bytes 24125440 | tf_op jit(solution)/shard_map/hqk,qhd->khd/dot_general | solution.py:18
  754.7 15.2 %multiply_reduce_fusion = (f32[4,512]{1,0:T(4,128)S(1)}, f32[4,512,2560]{2,1,0:T(8,128)}) fusion(f32[4,512,2560]{2,1,0:T(8,128)} %get-tuple-element.145, f32[4,512]{1,0:T(4,128)S(1)} %copy-done.48, bf16[512,4,128]{0,2,1:T(8,128)(2,1)} %bitcast.253, bf16[2560,4,256]{0,2,1:T(8,128)(2,1)} %bitcast.239), kind=kOutput, calls=%fused_computation.9 | convolution fusion | flops 1357903872 | bytes 45105152 | tf_op jit(solution)/shard_map/qhd,khd->hqk/dot_general | solution.py:18
  769.9 14.6 %multiply_convert_fusion = bf16[4,512,2560]{2,1,0:T(8,128)(2,1)S(1)} fusion(f32[4,512,2560]{2,1,0:T(8,128)} %get-tuple-element.150, f32[4,512]{1,0:T(4,128)S(1)} %get-tuple-element.149, f32[4,512,2560]{2,1,0:T(8,128)} %get-tuple-element.145, f32[4,512]{1,0:T(4,128)S(1)} %copy-done.48), kind=kLoop, calls=%fused_computation.8 | loop fusion | flops 20971520 | bytes 52445184 | tf_op jit(solution)/shard_map/convert_element_type | solution.py:232
  786.2 4.5 pad_maximum_fusion.2
  793.5 2.9 fusion.174
  799.6 2.9 fusion.167
  808.3 4.2 fusion.113
  813.2 6.0 fusion.110
  820.5 3.2 convolution_convert_fusion.9
  823.8 2.5 fusion.119
  826.3 5.8 add_convert_fusion.2
  832.2 3.6 convolution_convert_fusion.4
  839.3 4.1 pad_maximum_fusion
  843.4 7.2 fusion.92
  850.6 2.6 reshape.312
  855.6 5.6 convolution_convert_fusion.3
  861.3 3.5 convolution_convert_fusion.8
  864.7 178.7 %all-reduce.10.cloned.1.call-done = (bf16[512,2048]{1,0:T(8,128)(2,1)}, bf16[512,2048]{1,0:T(8,128)(2,1)}, bf16[512,576]{0,1:T(8,128)(2,1)}, bf16[2048,64]{0,1:T(8,128)(2,1)}) async-done(((bf16[512,2048]{1,0:T(8,128)(2,1)}, bf16[512,2048]{1,0:T(8,128)(2,1)}, bf16[512,576]{0,1:T(8,128)(2,1)}, bf16[2048,64]{0,1:T(8,128)(2,1)}), (bf16[512,2048]{1,0:T(8,128)(2,1)}, bf16[512,2048]{1,0:T(8,128)(2,1)}, ...) | async-done | bytes 5046288 | tf_op jit(solution)/shard_map/psum | solution.py:272
  1047.5 6.6 fusion.63
  1054.4 4.7 convolution_convert_fusion.7
  1059.2 40.1 %concatenate.47 = bf16[2048,2179]{0,1:T(8,128)(2,1)} concatenate(bf16[2048,512]{0,1:T(8,128)(2,1)} %convolution_convert_fusion.8, bf16[2048,768]{0,1:T(8,128)(2,1)} %convolution_convert_fusion.3, bf16[2048,576]{0,1:T(8,128)(2,1)} %convolution_convert_fusion.7, bf16[2048,256]{0,1:T(8,128)(2,1)} %copy.126, bf16[2048,64]{0,1:T(8,128)(2,1)S(1)} %copy-done.39, ...), dimensions={1} | concatenate | bytes 17850368 | tf_op jit(solution)/shard_map/concatenate | solution.py:66
  1099.3 2.6 convert_bitcast_fusion
  1101.9 21.4 %convolution_bitcast_fusion = f32[8,2048,352]{1,2,0:T(8,128)} fusion(bf16[8,8,72,2048]{3,2,1,0:T(8,128)(2,1)} %convolution_convert_fusion.1, bf16[8,8,72,352]{3,2,0,1:T(8,128)(2,1)} %get-tuple-element.114), kind=kOutput, calls=%fused_computation.53 | convolution fusion | flops 6643777536 | bytes 45187072 | tf_op jit(solution)/shard_map/becd,becf->edf/dot_general | solution.py:18
  1123.3 22.3 %convolution_bitcast_fusion.1 = f32[8,2048,352]{1,2,0:T(8,128)} fusion(bf16[8,8,72,2048]{3,2,1,0:T(8,128)(2,1)} %convolution_convert_fusion.1, bf16[8,8,72,352]{3,2,0,1:T(8,128)(2,1)S(1)} %copy-done.8), kind=kOutput, calls=%fused_computation.54 | convolution fusion | flops 6643777536 | bytes 45187072 | tf_op jit(solution)/shard_map/becd,becf->edf/dot_general | solution.py:18
  1145.6 18.2 %fusion.35 = f32[8,352,2048]{2,1,0:T(8,128)} fusion(bf16[8,8,72,352]{3,2,0,1:T(8,128)(2,1)} %get-tuple-element.136, bf16[8,8,72,2048]{3,2,1,0:T(8,128)(2,1)} %convolution_convert_fusion), kind=kOutput, calls=%fused_computation.52 | convolution fusion | flops 6643777536 | bytes 45187072 | tf_op jit(solution)/shard_map/becf,becd->efd/dot_general | solution.py:18
  1163.7 8.7 fusion.66
  (267 shorter events, 72.1 us)
Async XLA Ops:
  8.0 28.3 %copy-start = (bf16[2048,768]{1,0:T(8,128)(2,1)S(1)}, bf16[2048,768]{1,0:T(8,128)(2,1)}, u32[]{:S(2)}) copy-start(bf16[2048,768]{1,0:T(8,128)(2,1)} %param.23) | copy-start | bytes 9437188
  8.0 224.8 %all-reduce.6.cloned.1.call-start = ((), (), s32[]{:S(2)}) async-start(), calls=%async_computation.4 | async-start | bytes 4194304 | tf_op jit(solution)/shard_map/psum | solution.py:147
  8.1 9.3 copy-start.65
  10.7 6.7 copy-start.50
  13.4 22.9 %copy-start.63 = (f32[512]{0:T(512)}, f32[512]{0:T(512)S(1)}, u32[]{:S(2)}) copy-start(f32[512]{0:T(512)S(1)} %fusion.148) | copy-start | bytes 6148
  13.4 5.7 copy-start.58
  17.2 17.8 %copy-start.49 = (s32[4096]{0:T(1024)S(1)}, s32[4096]{0:T(1024)}, u32[]{:S(2)}) copy-start(s32[4096]{0:T(1024)} %param.19) | copy-start | bytes 49156
  17.2 19.0 %copy-start.61 = (f32[2048]{0:T(1024)S(1)}, f32[2048]{0:T(1024)}, u32[]{:S(2)}) copy-start(f32[2048]{0:T(1024)} %param.22) | copy-start | bytes 24580
  19.0 20.8 %copy-start.35 = (f32[512,32]{0,1:T(8,128)}, f32[512,32]{0,1:T(8,128)S(1)}, u32[]{:S(2)}) copy-start(f32[512,32]{0,1:T(8,128)S(1)} %get-tuple-element.143) | copy-start | bytes 196612
  20.9 44.2 %collective-permute-start = (bf16[512,576]{0,1:T(8,128)(2,1)}, bf16[512,576]{0,1:T(8,128)(2,1)}, u32[]{:S(2)}, u32[]{:S(2)}) collective-permute-start(bf16[512,576]{0,1:T(8,128)(2,1)} %pad_maximum_fusion.4), channel_id=1, source_target_pairs={{0,16},{4,20},{8,24},{12,28},{1,17},{5,21},{9,25},{13,29},{2,18},{... | collective-permute-start | bytes 1769480 | tf_op jit(solution)/shard_map/ppermute | solution.py:24
  26.6 39.6 %collective-permute-start.1 = (bf16[512,576]{0,1:T(8,128)(2,1)}, bf16[512,576]{0,1:T(8,128)(2,1)}, u32[]{:S(2)}, u32[]{:S(2)}) collective-permute-start(bf16[512,576]{0,1:T(8,128)(2,1)} %pad_maximum_fusion.4), channel_id=1, source_target_pairs={{0,12},{4,16},{8,20},{12,24},{16,28},{1,13},{5,17},{9,21},{13,25},... | collective-permute-start | bytes 1769480 | tf_op jit(solution)/shard_map/ppermute | solution.py:24
  29.9 37.3 %collective-permute-start.2 = (bf16[512,576]{0,1:T(8,128)(2,1)}, bf16[512,576]{0,1:T(8,128)(2,1)}, u32[]{:S(2)}, u32[]{:S(2)}) collective-permute-start(bf16[512,576]{0,1:T(8,128)(2,1)} %pad_maximum_fusion.4), channel_id=1, source_target_pairs={{0,8},{4,12},{8,16},{12,20},{16,24},{20,28},{1,9},{5,13},{9,17},{1... | collective-permute-start | bytes 1769480 | tf_op jit(solution)/shard_map/ppermute | solution.py:24
  32.9 35.5 %collective-permute-start.3 = (bf16[512,576]{0,1:T(8,128)(2,1)}, bf16[512,576]{0,1:T(8,128)(2,1)}, u32[]{:S(2)}, u32[]{:S(2)}) collective-permute-start(bf16[512,576]{0,1:T(8,128)(2,1)} %pad_maximum_fusion.4), channel_id=1, source_target_pairs={{0,4},{4,8},{8,12},{12,16},{16,20},{20,24},{24,28},{1,5},{5,9},{9,... | collective-permute-start | bytes 1769480 | tf_op jit(solution)/shard_map/ppermute | solution.py:24
  39.8 33.2 %copy-start.22 = (f32[512,768]{0,1:T(8,128)}, f32[512,768]{0,1:T(8,128)S(1)}, u32[]{:S(2)}) copy-start(f32[512,768]{0,1:T(8,128)S(1)} %fusion.159) | copy-start | bytes 4718596
  39.8 29.7 %copy-start.21 = (bf16[512,512]{0,1:T(8,128)(2,1)S(1)}, bf16[512,512]{0,1:T(8,128)(2,1)}, u32[]{:S(2)}) copy-start(bf16[512,512]{0,1:T(8,128)(2,1)} %copy-done.20) | copy-start | bytes 1572868
  39.8 29.7 %copy-start.69 = (bf16[512,1024]{1,0:T(8,128)(2,1)S(1)}, bf16[512,1024]{1,0:T(8,128)(2,1)}, u32[]{:S(2)}) copy-start(bf16[512,1024]{1,0:T(8,128)(2,1)} %param.26) | copy-start | bytes 3145732
  39.9 42.0 %copy-start.27 = (bf16[512,4,32]{0,2,1:T(8,128)(2,1)}, bf16[512,4,32]{0,2,1:T(8,128)(2,1)S(1)}, u32[]{:S(2)}) copy-start(bf16[512,4,32]{0,2,1:T(8,128)(2,1)S(1)} %get-tuple-element.125) | copy-start | bytes 393220
  40.0 42.0 %copy-start.29 = (bf16[512,4,32]{0,2,1:T(8,128)(2,1)}, bf16[512,4,32]{0,2,1:T(8,128)(2,1)S(1)}, u32[]{:S(2)}) copy-start(bf16[512,4,32]{0,2,1:T(8,128)(2,1)S(1)} %get-tuple-element.126) | copy-start | bytes 393220
  73.0 9.0 copy-start.26
  119.1 17.4 %copy-start.47 = (f32[4,512]{1,0:T(4,128)}, f32[4,512]{1,0:T(4,128)S(1)}, u32[]{:S(2)}) copy-start(f32[4,512]{1,0:T(4,128)S(1)} %get-tuple-element.144) | copy-start | bytes 24580
  140.8 96.3 %copy-start.41 = (f32[2048]{0:T(1024)S(1)}, f32[2048]{0:T(1024)}, u32[]{:S(2)}) copy-start(f32[2048]{0:T(1024)} %param.28) | copy-start | bytes 24580
  140.9 111.8 %all-gather.5.cloned.1.call-start = ((), (), s32[]{:S(2)}) async-start(), calls=%async_computation.6 | async-start | bytes 18874368 | tf_op jit(solution)/shard_map/all_gather | solution.py:103
  141.4 189.2 %all-gather.3.cloned.1.call-start = ((), (), s32[]{:S(2)}) async-start(), calls=%async_computation.5 | async-start | bytes 18874368 | tf_op jit(solution)/shard_map/all_gather | solution.py:152
  239.6 391.3 %reduce-scatter.5.cloned.1.call-start = ((), (), s32[]{:S(2)}) async-start(), calls=%async_computation.7 | async-start | bytes 18874368 | tf_op jit(solution)/shard_map/reduce_scatter | solution.py:214
  389.9 25.7 %copy-start.31 = (bf16[2048,64]{0,1:T(8,128)(2,1)S(1)}, bf16[2048,64]{0,1:T(8,128)(2,1)}, u32[]{:S(2)}) copy-start(bf16[2048,64]{0,1:T(8,128)(2,1)} %param.29) | copy-start | bytes 786436
  415.6 14.2 %slice-start.2 = ((s8[7077888]{0:T(1024)(128)(4,1)}), s8[4194304]{0:T(1024)(128)(4,1)S(1)}, s32[]{:S(2)}) async-start(s8[7077888]{0:T(1024)(128)(4,1)} %bitcast.226), calls=%async_computation.15 | async-start | bytes 8388608
  415.6 14.2 %slice-start.4 = ((s8[7077888]{0:T(1024)(128)(4,1)}), s8[4194304]{0:T(1024)(128)(4,1)S(1)}, s32[]{:S(2)}) async-start(s8[7077888]{0:T(1024)(128)(4,1)} %bitcast.228), calls=%async_computation.17 | async-start | bytes 8388608
  415.6 14.2 %slice-start.6 = ((s8[7077888]{0:T(1024)(128)(4,1)}), s8[4194304]{0:T(1024)(128)(4,1)S(1)}, s32[]{:S(2)}) async-start(s8[7077888]{0:T(1024)(128)(4,1)} %bitcast.230), calls=%async_computation.19 | async-start | bytes 8388608
  415.6 14.2 %slice-start.3 = ((s8[7077888]{0:T(1024)(128)(4,1)}), s8[2883584]{0:T(1024)(128)(4,1)S(1)}, s32[]{:S(2)}) async-start(s8[7077888]{0:T(1024)(128)(4,1)} %bitcast.226), calls=%async_computation.16 | async-start | bytes 5767168
  415.6 14.2 %slice-start.5 = ((s8[7077888]{0:T(1024)(128)(4,1)}), s8[2883584]{0:T(1024)(128)(4,1)S(1)}, s32[]{:S(2)}) async-start(s8[7077888]{0:T(1024)(128)(4,1)} %bitcast.228), calls=%async_computation.18 | async-start | bytes 5767168
  415.6 14.2 %slice-start.7 = ((s8[7077888]{0:T(1024)(128)(4,1)}), s8[2883584]{0:T(1024)(128)(4,1)S(1)}, s32[]{:S(2)}) async-start(s8[7077888]{0:T(1024)(128)(4,1)} %bitcast.230), calls=%async_computation.20 | async-start | bytes 5767168
  514.9 209.8 %all-reduce.8.cloned.1.call-start = ((), (), s32[]{:S(2)}) async-start(), calls=%async_computation.9 | async-start | bytes 4194304 | tf_op jit(solution)/shard_map/psum | solution.py:215
  638.0 188.3 %reduce-scatter.7.cloned.1.call-start = ((), (), s32[]{:S(2)}) async-start(), calls=%async_computation.8 | async-start | bytes 18874368 | tf_op jit(solution)/shard_map/reduce_scatter | solution.py:218
  667.6 57.1 %copy-start.42 = (f32[2048]{0:T(1024)S(1)}, f32[2048]{0:T(1024)}, u32[]{:S(2)}) copy-start(f32[2048]{0:T(1024)} %param.28) | copy-start | bytes 24580
  667.6 57.1 %copy-start.44 = (f32[512]{0:T(512)S(1)}, f32[512]{0:T(512)}, u32[]{:S(2)}) copy-start(f32[512]{0:T(512)} %copy-done.43) | copy-start | bytes 6148
  667.6 375.7 %all-reduce.10.cloned.1.call-start = ((), (), s32[]{:S(2)}) async-start(), calls=%async_computation.12 | async-start | bytes 10092544 | tf_op jit(solution)/shard_map/psum | solution.py:272
  677.9 51.7 %copy-start.57 = (f32[512]{0:T(512)S(1)}, f32[512]{0:T(512)}, u32[]{:S(2)}) copy-start(f32[512]{0:T(512)} %copy-done.56) | copy-start | bytes 6148
  724.7 4.9 copy-start.6
  724.7 5.0 copy-start.12
  729.7 5.4 copy-start.48
  769.9 14.7 %copy-start.23 = (f32[512,768]{0,1:T(8,128)S(1)}, f32[512,768]{0,1:T(8,128)}, u32[]{:S(2)}) copy-start(f32[512,768]{0,1:T(8,128)} %copy-done.22) | copy-start | bytes 4718596
  802.5 21.2 %collective-permute-start.4 = (bf16[512,576]{0,1:T(8,128)(2,1)}, bf16[512,576]{0,1:T(8,128)(2,1)S(1)}, u32[]{:S(2)}, u32[]{:S(2)}) collective-permute-start(bf16[512,576]{0,1:T(8,128)(2,1)} %get-tuple-element.118), channel_id=1, source_target_pairs={{16,0},{20,4},{24,8},{28,12},{17,1},{21,5},{25,9},{29,13},{18,2},{... | collective-permute-start | bytes 1769480 | tf_op jit(solution)/shard_map/ppermute | solution.py:24
  803.8 19.9 %collective-permute-start.5 = (bf16[512,576]{0,1:T(8,128)(2,1)}, bf16[512,576]{0,1:T(8,128)(2,1)S(1)}, u32[]{:S(2)}, u32[]{:S(2)}) collective-permute-start(bf16[512,576]{0,1:T(8,128)(2,1)} %get-tuple-element.121), channel_id=1, source_target_pairs={{12,0},{16,4},{20,8},{24,12},{28,16},{13,1},{17,5},{21,9},{25,13},... | collective-permute-start | bytes 1769480 | tf_op jit(solution)/shard_map/ppermute | solution.py:24
  805.1 18.6 %collective-permute-start.6 = (bf16[512,576]{0,1:T(8,128)(2,1)}, bf16[512,576]{0,1:T(8,128)(2,1)}, u32[]{:S(2)}, u32[]{:S(2)}) collective-permute-start(bf16[512,576]{0,1:T(8,128)(2,1)} %get-tuple-element.120), channel_id=1, source_target_pairs={{8,0},{12,4},{16,8},{20,12},{24,16},{28,20},{9,1},{13,5},{17,9},{2... | collective-permute-start | bytes 1769480 | tf_op jit(solution)/shard_map/ppermute | solution.py:24
  806.4 6.1 copy-start.36
  806.4 6.1 copy-start.40
  806.4 17.3 %collective-permute-start.7 = (bf16[512,576]{0,1:T(8,128)(2,1)S(1)}, bf16[512,576]{0,1:T(8,128)(2,1)}, u32[]{:S(2)}, u32[]{:S(2)}) collective-permute-start(bf16[512,576]{0,1:T(8,128)(2,1)S(1)} %get-tuple-element.119), channel_id=1, source_target_pairs={{4,0},{8,4},{12,8},{16,12},{20,16},{24,20},{28,24},{5,1},{9,5},{13... | collective-permute-start | bytes 1769480 | tf_op jit(solution)/shard_map/ppermute | solution.py:24
  832.1 267.1 %reduce-scatter.11.cloned.1.call-start = ((), (), s32[]{:S(2)}) async-start(), calls=%async_computation.11 | async-start | bytes 9732096 | tf_op jit(solution)/shard_map/reduce_scatter | solution.py:67
  843.4 329.7 %reduce-scatter.9.cloned.1.call-start = ((), (), s32[]{:S(2)}) async-start(), calls=%async_computation.10 | async-start | bytes 10063872 | tf_op jit(solution)/shard_map/reduce_scatter | solution.py:67
  850.6 4.9 copy-start.62
  850.6 5.0 copy-start.64
  855.6 5.6 copy-start.3
  855.6 5.6 copy-start.7
  855.6 5.6 copy-start.13
  855.6 5.6 copy-start.16
  855.6 5.6 copy-start.71
  861.2 183.5 %copy-start.46 = (f32[512]{0:T(512)S(1)}, f32[512]{0:T(512)}, u32[]{:S(2)}) copy-start(f32[512]{0:T(512)} %copy-done.45) | copy-start | bytes 6148
  861.2 183.5 %copy-start.59 = (f32[512]{0:T(512)S(1)}, f32[512]{0:T(512)}, u32[]{:S(2)}) copy-start(f32[512]{0:T(512)} %param.25) | copy-start | bytes 6148
  861.2 185.6 %copy-start.55 = (f32[512]{0:T(512)S(1)}, f32[512]{0:T(512)}, u32[]{:S(2)}) copy-start(f32[512]{0:T(512)} %copy-done.54) | copy-start | bytes 6148
  861.2 185.6 %copy-start.51 = (f32[512]{0:T(512)S(1)}, f32[512]{0:T(512)}, u32[]{:S(2)}) copy-start(f32[512]{0:T(512)} %copy-done.50) | copy-start | bytes 6148
  861.2 185.6 %copy-start.66 = (f32[32]{0:T(128)S(1)}, f32[32]{0:T(128)}, u32[]{:S(2)}) copy-start(f32[32]{0:T(128)} %copy-done.65) | copy-start | bytes 388
  1047.5 6.6 copy-start.38
  1101.9 21.4 %copy-start.8 = (bf16[8,8,72,352]{3,2,0,1:T(8,128)(2,1)S(1)}, bf16[8,8,72,352]{3,2,0,1:T(8,128)(2,1)}, u32[]{:S(2)}) copy-start(bf16[8,8,72,352]{3,2,0,1:T(8,128)(2,1)} %get-tuple-element.115) | copy-start | bytes 9732100
  1145.5 18.2 %copy-start.53 = (f32[512]{0:T(512)S(1)}, f32[512]{0:T(512)}, u32[]{:S(2)}) copy-start(f32[512]{0:T(512)} %copy-done.52) | copy-start | bytes 6148
  (34 other events, 100.8 us)
Sparse Core Ops, SparseCore 0:
  141.0 91.8 all-reduce.5
  638.1 86.5 all-reduce.7
  832.3 211.0 all-reduce.9
Sparse Core Ops, SparseCore 1:
  143.4 95.0 all-gather.4
  240.9 89.7 all-gather.2
  515.0 115.8 reduce-scatter.4
  667.7 115.8 reduce-scatter.6
  843.5 99.9 reduce-scatter.10
  1099.3 73.7 reduce-scatter.8
where the time goes:
time: 1200 us
  waiting for transfers between devices  498 us (42%)
  matrix products  471 us (39%)
  other arithmetic  111 us (9%)
  local copies, waits for them, and re-layouts  67.1 us (6%)
  starting transfers between devices  20.8 us (2%)
  between operations  16.7 us (1%)
    dot_general x38, matrix products, dot(): return jnp.einsum(eq, a, b, preferred_element_type=F32)  433 us
    psum x1, waiting for transfers between devices, shards(): lax.psum((routed_block.astype(F32) + shared_result).astype(BF), 'tensor')  179 us
    reduce_scatter x1, waiting for transfers between devices, shards(): lax.psum_scatter(mid_part.astype(BF), 'dp', scatter_dimension=0, tiled=True)  95.9 us
    psum x1, waiting for transfers between devices, shards(): lax.psum(jnp.dot(attended, w_out, preferred_element_type=F32).astype(BF),...  91.4 us
    all_gather x1, waiting for transfers between devices, shards(): hidden_all = lax.all_gather(hidden_mid, 'dp', tiled=True)  59.2 us
    psum x1, waiting for transfers between devices, shards(): lax.psum((mid_block.astype(F32) + mid_from_shared).astype(BF), 'tensor')  46.8 us
    concatenate x1, local copies, waits for them, and re-layouts, scatter_sum(): joined = jnp.concatenate(parts, axis=1)  40.1 us
    ppermute x8, waiting for transfers between devices, passed_along(): return lax.ppermute(shard, axis, pairs)  25.1 us
  transfers between devices with their start and end apart: 17, of which 7 were waited for; matrix products, arithmetic and copies ran while one was open for 29% of the time, Pallas kernels for 0%

commit v1 on v0

--- a/solution.py
+++ b/solution.py
@@ -12,6 +12,24 @@
 BF = jnp.bfloat16
 F32 = jnp.float32
 epsilon = 1e-06
+
+
+def joined_along(blocks, dim):
+    blocks = jnp.moveaxis(blocks, 0, dim)
+    shape = blocks.shape
+    return blocks.reshape(*shape[:dim], shape[dim] * shape[dim + 1], *shape[dim + 2 :])
+
+
+def collected_by_bits(x, axis):
+    devices = lax.axis_size(axis)
+    tiles = x[None]
+    for level in range(devices.bit_length() - 1):
+        stride = 1 << level
+        theirs = lax.ppermute(tiles, axis, [(i, i ^ stride) for i in range(devices)])
+        both = jnp.stack([tiles, theirs])
+        upper = lax.axis_index(axis) >> level & 1
+        tiles = jnp.where(upper == 0, both, both[::-1]).reshape(-1, *x.shape)
+    return tiles
 
 
 def dot(eq, a, b):
@@ -149,7 +167,7 @@
     ).astype(F32)
     middle = token_features + attention
     hidden_mid = normed(middle, middle_gain).astype(BF)
-    hidden_all = lax.all_gather(hidden_mid, "dp", tiled=True)
+    hidden_all = joined_along(collected_by_bits(hidden_mid, "dp"), 0)
     shared_gate_val = jnp.dot(hidden_mid, shared_gate, preferred_element_type=F32)
     shared_up_val = jnp.dot(hidden_mid, shared_up, preferred_element_type=F32)
     shared_active = silu_gate(shared_gate_val, shared_up_val).astype(BF)

time: 1200 us -> 1480 us (1.23)
  blocking collectives: 9.42 us -> 185 us
  other arithmetic: 111 us -> 175 us
  waiting for transfers between devices: 498 us -> 531 us
    all_gather x1, blocking collectives: 9.42 us -> 185 us  [shards(): route_all = lax.all_gather(route_ids, 'dp', tiled=True)]
    ppermute x0 -> x3, waiting for transfers between devices: none -> 95.9 us  [collected_by_bits(): lax.ppermute(tiles, axis, [(i, i ^ stride) for i in range(devices)])]
    all_gather x1 -> x0, waiting for transfers between devices: 59.2 us -> none  [shards(): hidden_all = lax.all_gather(hidden_mid, 'dp', tiled=True)]
    another operation x5 -> x9, other arithmetic: 3.56 us -> 32.6 us  [the longest x4 29 us: collected_by_bits(): both = jnp.stack([tiles, theirs])]
    select_n x0 -> x2, other arithmetic: none -> 28.2 us  [collected_by_bits(): tiles = jnp.where(upper == 0, both, both[::-1]).reshape(-1, *x.shape)]
  transfers between devices with their start and end apart: 17 -> 19, of which waited for: 7 -> 9; matrix products, arithmetic and copies ran while one was open for 29% -> 31% of each run, Pallas kernels for 0% -> 0%
where the time goes in v1:
time: 1480 us; the launch traced here: 1470 us
  waiting for transfers between devices  531 us (36%)
  matrix products  470 us (32%)
  blocking collectives  185 us (12%)
  other arithmetic  175 us (12%)
  local copies, waits for them, and re-layouts  68.6 us (5%)
  starting transfers between devices  24.1 us (2%)
  between operations  16.7 us (1%)
    dot_general x38, matrix products, dot(): return jnp.einsum(eq, a, b, preferred_element_type=F32)  435 us
    all_gather x1, blocking collectives, shards(): route_all = lax.all_gather(route_ids, 'dp', tiled=True)  185 us
    psum x1, waiting for transfers between devices, shards(): lax.psum((routed_block.astype(F32) + shared_result).astype(BF), 'tensor')  171 us
    ppermute x3, waiting for transfers between devices, collected_by_bits(): lax.ppermute(tiles, axis, [(i, i ^ stride) for i in range(devices)])  95.9 us
    reduce_scatter x1, waiting for transfers between devices, shards(): lax.psum_scatter(mid_part.astype(BF), 'dp', scatter_dimension=0, tiled=True)  93.6 us
    psum x1, waiting for transfers between devices, shards(): lax.psum(jnp.dot(attended, w_out, preferred_element_type=F32).astype(BF),...  90.8 us
    psum x1, waiting for transfers between devices, shards(): lax.psum((mid_block.astype(F32) + mid_from_shared).astype(BF), 'tensor')  46.4 us
    concatenate x1, local copies, waits for them, and re-layouts, scatter_sum(): joined = jnp.concatenate(parts, axis=1)  40.2 us
  transfers between devices with their start and end apart: 19, of which 9 were waited for; matrix products, arithmetic and copies ran while one was open for 31% of the time, Pallas kernels for 0%

profile of v1, /device:TPU:0, one launch (start us, length us, event | category | flops | bytes accessed | tf_op | source)
XLA Modules:
  0.0 1469.8 jit_solution(14222011815443711639)
XLA Ops:
  13.4 3.8 fusion.163
  20.9 5.7 collective-permute-start
  26.6 3.4 collective-permute-start.1
  36.4 3.5 fusion.161
  40.0 25.1 %collective-permute-done = bf16[512,576]{0,1:T(8,128)(2,1)} collective-permute-done((bf16[512,576]{0,1:T(8,128)(2,1)}, bf16[512,576]{0,1:T(8,128)(2,1)}, u32[]{:S(2)}, u32[]{:S(2)}) %collective-permute-start) | collective-permute-done | bytes 589856 | tf_op jit(solution)/shard_map/ppermute | solution.py:42
  69.7 3.5 convolution_convert_fusion.2
  73.2 8.9 fusion.84
  82.2 13.6 fusion.3
  95.8 23.7 %fusion.171 = (f32[4,512]{1,0:T(4,128)S(1)}, f32[4,512,2560]{2,1,0:T(8,128)}) fusion(f32[4,512,2560]{2,1,0:T(8,128)} %fusion.3), kind=kOutput, calls=%fused_computation.259 | output fusion | flops 10488319 | bytes 41951232 | tf_op jit(solution)/shard_map/sub | solution.py:160
  119.5 17.4 %fusion.107 = bf16[4,128,512]{2,1,0:T(8,128)(2,1)} fusion(bf16[2560,4,256]{0,2,1:T(8,128)(2,1)} %bitcast.248, f32[4,512]{1,0:T(4,128)S(1)} %get-tuple-element.146, f32[4,512,2560]{2,1,0:T(8,128)} %fusion.3), kind=kOutput, calls=%fused_computation.155 | convolution fusion | flops 1358172672 | bytes 45096960 | tf_op jit(solution)/shard_map/hqk,khd->qhd/dot_general | solution.py:36
  136.9 4.4 convolution_convert_fusion.10
  142.4 90.8 %all-reduce.6.cloned.1.call-done = bf16[512,2048]{1,0:T(8,128)(2,1)} async-done(((bf16[512,2048]{1,0:T(8,128)(2,1)}), bf16[512,2048]{1,0:T(8,128)(2,1)}) %all-reduce.6.cloned.1.call-update) | async-done | bytes 2097168 | tf_op jit(solution)/shard_map/psum | solution.py:165
  239.4 4.5 collective-permute-done.4
  246.5 5.0 fusion.77
  252.9 91.4 %collective-permute-done.5 = bf16[2,512,2048]{2,1,0:T(8,128)(2,1)} collective-permute-done((bf16[2,512,2048]{2,1,0:T(8,128)(2,1)}, bf16[2,512,2048]{2,1,0:T(8,128)(2,1)}, u32[]{:S(2)}, u32[]{:S(2)}) %collective-permute-start.5) | collective-permute-done | bytes 4194336 | tf_op jit(solution)/shard_map/ppermute | solution.py:28
  344.4 7.6 pad_maximum_fusion.2
  352.0 14.2 reverse_select_fusion.1
  367.6 184.8 %all_gather.6 = s32[4096,6]{0,1:T(8,128)S(1)} all-gather(s32[512,6]{0,1:T(8,128)S(1)} %copy-done.62), channel_id=1, replica_groups=mesh['dp'=8,'tensor'=4] {'dp'}, dimensions={0}, use_global_device_ids=true | all-gather | bytes 110592 | tf_op jit(solution)/shard_map/all_gather | solution.py:122
  556.0 13.8 pad_maximum_fusion
  569.8 14.0 reverse_select_fusion
  583.9 5.2 fusion.172
  591.2 18.8 %convolution_convert_fusion.1 = bf16[8,8,72,2048]{3,2,1,0:T(8,128)(2,1)} fusion(bf16[8,512,2048,1]{2,1,3,0:T(8,128)(2,1)} %bitcast.235, s32[8,8,512]{2,1,0:T(8,128)S(1)} %fusion.122), kind=kOutput, calls=%fused_computation.29 | convolution fusion | flops 9675472896 | bytes 35782656 | tf_op jit(solution)/shard_map/bect,btd->becd/dot_general | solution.py:36
  610.0 20.2 %fusion.18 = f32[8,8,72,352]{3,2,1,0:T(8,128)} fusion(bf16[8,8,72,2048]{3,2,1,0:T(8,128)(2,1)} %convolution_convert_fusion.1, bf16[8,2048,352]{1,2,0:T(8,128)(2,1)} %param.31), kind=kOutput, calls=%fused_computation.24 | convolution fusion | flops 6643777536 | bytes 36896768 | tf_op jit(solution)/shard_map/becd,edf->becf/dot_general | solution.py:36
  630.2 20.0 %fusion.20 = f32[8,8,72,352]{3,2,1,0:T(8,128)} fusion(bf16[8,8,72,2048]{3,2,1,0:T(8,128)(2,1)} %convolution_convert_fusion.1, bf16[8,2048,352]{1,2,0:T(8,128)(2,1)} %param.30), kind=kOutput, calls=%fused_computation.26 | convolution fusion | flops 6643777536 | bytes 36896768 | tf_op jit(solution)/shard_map/becd,edf->becf/dot_general | solution.py:36
  650.3 18.7 %convolution_convert_fusion = bf16[8,8,72,2048]{3,2,1,0:T(8,128)(2,1)} fusion(bf16[8,512,2048,1]{2,1,3,0:T(8,128)(2,1)} %bitcast.259, s32[8,8,512]{2,1,0:T(8,128)S(1)} %fusion.122), kind=kOutput, calls=%fused_computation.28 | convolution fusion | flops 9675472896 | bytes 35782656 | tf_op jit(solution)/shard_map/bect,btd->becd/dot_general | solution.py:36
  669.0 24.5 %fusion.39 = (bf16[8,8,72]{2,0,1:T(8,128)(2,1)S(1)}, bf16[8,8,72,352]{3,2,0,1:T(8,128)(2,1)}, f32[8,8,72,352]{3,2,1,0:T(8,128)}) fusion(f32[8,8,72,352]{3,2,1,0:T(8,128)} %fusion.18, f32[8,8,72,352]{3,2,1,0:T(8,128)} %fusion.20, bf16[8,352,2048]{2,1,0:T(8,128)(2,1)} %param.32, bf16[8,8,72,2048]{3,2,1,0:T(8,128)(2,1)} %convolution_convert_fusion), kind=kOutput, calls=%fused_computation.60 | convolution fusion | flops 6658371072 | bytes 53126144 | tf_op jit(solution)/shard_map/becd,efd->becf/dot_general | solution.py:36
  698.2 12.9 multiply_convert_fusion.1
  711.1 21.2 %fusion.31 = f32[8,8,72,2048]{3,2,0,1:T(8,128)} fusion(bf16[8,2048,352]{1,2,0:T(8,128)(2,1)} %param.30, bf16[8,8,72,352]{3,2,0,1:T(8,128)(2,1)} %get-tuple-element.115), kind=kOutput, calls=%fused_computation.36 | convolution fusion | flops 6643777536 | bytes 52527104 | tf_op jit(solution)/shard_map/becf,edf->becd/dot_general | solution.py:36
  732.3 40.2 %fusion.5 = f32[8,512,2048,1]{2,1,3,0:T(8,128)} fusion(f32[8,8,72,2048]{3,2,0,1:T(8,128)} %fusion.31, bf16[8,2048,352]{1,2,0:T(8,128)(2,1)} %param.31, bf16[8,8,72,352]{3,2,0,1:T(8,128)(2,1)} %get-tuple-element.114, pred[8,8,72,512]{3,2,1,0:T(8,128)(4,1)} %iota_compare_fusion.14), kind=kOutput, calls=%fused_computation.13 | convolution fusion | flops 16326328320 | bytes 88440832 | tf_op jit(solution)/shard_map/bect,becd->btd/dot_general | solution.py:36
  772.5 17.1 %fusion.1 = bf16[4096,2048]{1,0:T(8,128)(2,1)} fusion(f32[8,512,2048,1]{2,1,3,0:T(8,128)} %fusion.5, bf16[4096,64]{0,1:T(8,128)(2,1)} %multiply_convert_fusion.6, bf16[2048,64]{0,1:T(8,128)(2,1)S(1)} %copy-done.33), kind=kOutput, calls=%fused_computation.3 | convolution fusion | flops 1090519040 | bytes 51118080 | tf_op jit(solution)/shard_map/te,de->td/dot_general | solution.py:36
  792.9 4.8 fusion.173
  797.7 4.0 fusion.174
  802.1 3.3 multiply_convert_fusion.5
  806.3 4.2 fusion.175
  810.5 93.6 %reduce-scatter.5.cloned.1.call-done = bf16[512,2048]{1,0:T(8,128)(2,1)} async-done(((bf16[4096,2048]{1,0:T(8,128)(2,1)}), bf16[512,2048]{1,0:T(8,128)(2,1)}) %reduce-scatter.5.cloned.1.call-update) | async-done | bytes 2097168 | tf_op jit(solution)/shard_map/reduce_scatter | solution.py:232
  904.1 7.1 add_convert_fusion.3
  911.7 29.4 %bitcast_convert_fusion = bf16[8,512,2048]{2,1,0:T(8,128)(2,1)} fusion(bf16[8,352,2048]{2,1,0:T(8,128)(2,1)} %param.32, bf16[8,8,72,352]{3,2,0,1:T(8,128)(2,1)} %get-tuple-element.138, pred[8,8,72,512]{3,2,1,0:T(8,128)(4,1)} %iota_compare_fusion.13), kind=kOutput, calls=%fused_computation.4 | convolution fusion | flops 16325279744 | bytes 33914880 | tf_op jit(solution)/shard_map/bect,becd->btd/dot_general | solution.py:36
  941.2 10.2 convolution_convert_fusion.11
  951.4 46.4 %all-reduce.8.cloned.1.call-done = bf16[512,2048]{1,0:T(8,128)(2,1)} async-done(((bf16[512,2048]{1,0:T(8,128)(2,1)}), bf16[512,2048]{1,0:T(8,128)(2,1)}) %all-reduce.8.cloned.1.call-update) | async-done | bytes 2097168 | tf_op jit(solution)/shard_map/psum | solution.py:233
  997.9 4.8 multiply_reduce_fusion.2
  1002.9 5.4 convolution_convert_fusion.12
  1008.3 19.6 %fusion.69 = bf16[2560,4,128]{0,2,1:T(8,128)(2,1)} fusion(bf16[512,4,128]{0,2,1:T(8,128)(2,1)} %bitcast.262, f32[4,512]{1,0:T(4,128)S(1)} %copy-done.50, f32[4,512,2560]{2,1,0:T(8,128)} %fusion.3), kind=kOutput, calls=%fused_computation.112 | convolution fusion | flops 1359221248 | bytes 24125440 | tf_op jit(solution)/shard_map/hqk,qhd->khd/dot_general | solution.py:36
  1028.0 15.2 %multiply_reduce_fusion = (f32[4,512]{1,0:T(4,128)S(1)}, f32[4,512,2560]{2,1,0:T(8,128)}) fusion(f32[4,512,2560]{2,1,0:T(8,128)} %get-tuple-element.147, f32[4,512]{1,0:T(4,128)S(1)} %copy-done.50, bf16[512,4,128]{0,2,1:T(8,128)(2,1)} %bitcast.263, bf16[2560,4,256]{0,2,1:T(8,128)(2,1)} %bitcast.249), kind=kOutput, calls=%fused_computation.10 | convolution fusion | flops 1357903872 | bytes 45105152 | tf_op jit(solution)/shard_map/qhd,khd->hqk/dot_general | solution.py:36
  1043.2 14.7 multiply_convert_fusion
  1059.4 4.5 pad_maximum_fusion.4
  1081.3 4.2 fusion.115
  1086.2 6.0 fusion.112
  1093.6 3.2 convolution_convert_fusion.9
  1096.7 6.3 collective-permute-done.9
  1105.5 5.8 add_convert_fusion.2
  1111.5 3.5 convolution_convert_fusion.4
  1115.0 3.4 convolution_convert_fusion.5
  1120.1 4.1 pad_maximum_fusion.1
  1124.3 7.2 fusion.94
  1136.7 5.6 convolution_convert_fusion.3
  1143.0 3.5 convolution_convert_fusion.8
  1146.5 171.4 %all-reduce.10.cloned.1.call-done = (bf16[512,2048]{1,0:T(8,128)(2,1)}, bf16[512,2048]{1,0:T(8,128)(2,1)}, bf16[512,576]{0,1:T(8,128)(2,1)}, bf16[2048,64]{0,1:T(8,128)(2,1)}) async-done(((bf16[512,2048]{1,0:T(8,128)(2,1)}, bf16[512,2048]{1,0:T(8,128)(2,1)}, bf16[512,576]{0,1:T(8,128)(2,1)}, bf16[2048,64]{0,1:T(8,128)(2,1)}), (bf16[512,2048]{1,0:T(8,128)(2,1)}, bf16[512,2048]{1,0:T(8,128)(2,1)}, ...) | async-done | bytes 5046288 | tf_op jit(solution)/shard_map/psum | solution.py:290
  1322.0 6.6 fusion.63
  1328.9 4.7 convolution_convert_fusion.7
  1333.7 40.2 %concatenate.47 = bf16[2048,2179]{0,1:T(8,128)(2,1)} concatenate(bf16[2048,512]{0,1:T(8,128)(2,1)} %convolution_convert_fusion.8, bf16[2048,768]{0,1:T(8,128)(2,1)} %convolution_convert_fusion.3, bf16[2048,576]{0,1:T(8,128)(2,1)} %convolution_convert_fusion.7, bf16[2048,256]{0,1:T(8,128)(2,1)} %copy.126, bf16[2048,64]{0,1:T(8,128)(2,1)S(1)} %copy-done.41, ...), dimensions={1} | concatenate | bytes 17850368 | tf_op jit(solution)/shard_map/concatenate | solution.py:84
  1376.5 21.4 %convolution_bitcast_fusion = f32[8,2048,352]{1,2,0:T(8,128)} fusion(bf16[8,8,72,2048]{3,2,1,0:T(8,128)(2,1)} %convolution_convert_fusion.1, bf16[8,8,72,352]{3,2,0,1:T(8,128)(2,1)} %get-tuple-element.114), kind=kOutput, calls=%fused_computation.57 | convolution fusion | flops 6643777536 | bytes 45187072 | tf_op jit(solution)/shard_map/becd,becf->edf/dot_general | solution.py:36
  1397.9 22.3 %convolution_bitcast_fusion.1 = f32[8,2048,352]{1,2,0:T(8,128)} fusion(bf16[8,8,72,2048]{3,2,1,0:T(8,128)(2,1)} %convolution_convert_fusion.1, bf16[8,8,72,352]{3,2,0,1:T(8,128)(2,1)S(1)} %copy-done.9), kind=kOutput, calls=%fused_computation.58 | convolution fusion | flops 6643777536 | bytes 45187072 | tf_op jit(solution)/shard_map/becd,becf->edf/dot_general | solution.py:36
  1420.2 18.2 %fusion.35 = f32[8,352,2048]{2,1,0:T(8,128)} fusion(bf16[8,8,72,352]{3,2,0,1:T(8,128)(2,1)} %get-tuple-element.138, bf16[8,8,72,2048]{3,2,1,0:T(8,128)(2,1)} %convolution_convert_fusion), kind=kOutput, calls=%fused_computation.56 | convolution fusion | flops 6643777536 | bytes 45187072 | tf_op jit(solution)/shard_map/becf,becd->efd/dot_general | solution.py:36
  1438.4 8.7 fusion.66
  (265 shorter events, 101.5 us)
Async XLA Ops:
  8.0 28.3 %copy-start = (bf16[2048,768]{1,0:T(8,128)(2,1)S(1)}, bf16[2048,768]{1,0:T(8,128)(2,1)}, u32[]{:S(2)}) copy-start(bf16[2048,768]{1,0:T(8,128)(2,1)} %param.23) | copy-start | bytes 9437188
  8.0 225.2 %all-reduce.6.cloned.1.call-start = ((), (), s32[]{:S(2)}) async-start(), calls=%async_computation.4 | async-start | bytes 4194304 | tf_op jit(solution)/shard_map/psum | solution.py:165
  8.1 9.3 copy-start.67
  10.7 6.7 copy-start.52
  13.4 22.9 %copy-start.65 = (f32[512]{0:T(512)}, f32[512]{0:T(512)S(1)}, u32[]{:S(2)}) copy-start(f32[512]{0:T(512)S(1)} %fusion.150) | copy-start | bytes 6148
  13.4 5.7 copy-start.60
  17.2 17.9 %copy-start.51 = (s32[4096]{0:T(1024)S(1)}, s32[4096]{0:T(1024)}, u32[]{:S(2)}) copy-start(s32[4096]{0:T(1024)} %param.19) | copy-start | bytes 49156
  17.2 19.1 %copy-start.63 = (f32[2048]{0:T(1024)S(1)}, f32[2048]{0:T(1024)}, u32[]{:S(2)}) copy-start(f32[2048]{0:T(1024)} %param.22) | copy-start | bytes 24580
  19.1 20.8 %copy-start.37 = (f32[512,32]{0,1:T(8,128)}, f32[512,32]{0,1:T(8,128)S(1)}, u32[]{:S(2)}) copy-start(f32[512,32]{0,1:T(8,128)S(1)} %get-tuple-element.145) | copy-start | bytes 196612
  20.9 44.2 %collective-permute-start = (bf16[512,576]{0,1:T(8,128)(2,1)}, bf16[512,576]{0,1:T(8,128)(2,1)}, u32[]{:S(2)}, u32[]{:S(2)}) collective-permute-start(bf16[512,576]{0,1:T(8,128)(2,1)} %pad_maximum_fusion.7), channel_id=1, source_target_pairs={{0,16},{4,20},{8,24},{12,28},{1,17},{5,21},{9,25},{13,29},{2,18},{... | collective-permute-start | bytes 1769480 | tf_op jit(solution)/shard_map/ppermute | solution.py:42
  26.6 39.6 %collective-permute-start.1 = (bf16[512,576]{0,1:T(8,128)(2,1)}, bf16[512,576]{0,1:T(8,128)(2,1)}, u32[]{:S(2)}, u32[]{:S(2)}) collective-permute-start(bf16[512,576]{0,1:T(8,128)(2,1)} %pad_maximum_fusion.7), channel_id=1, source_target_pairs={{0,12},{4,16},{8,20},{12,24},{16,28},{1,13},{5,17},{9,21},{13,25},... | collective-permute-start | bytes 1769480 | tf_op jit(solution)/shard_map/ppermute | solution.py:42
  30.0 37.3 %collective-permute-start.2 = (bf16[512,576]{0,1:T(8,128)(2,1)}, bf16[512,576]{0,1:T(8,128)(2,1)}, u32[]{:S(2)}, u32[]{:S(2)}) collective-permute-start(bf16[512,576]{0,1:T(8,128)(2,1)} %pad_maximum_fusion.7), channel_id=1, source_target_pairs={{0,8},{4,12},{8,16},{12,20},{16,24},{20,28},{1,9},{5,13},{9,17},{1... | collective-permute-start | bytes 1769480 | tf_op jit(solution)/shard_map/ppermute | solution.py:42
  33.0 35.5 %collective-permute-start.3 = (bf16[512,576]{0,1:T(8,128)(2,1)}, bf16[512,576]{0,1:T(8,128)(2,1)}, u32[]{:S(2)}, u32[]{:S(2)}) collective-permute-start(bf16[512,576]{0,1:T(8,128)(2,1)} %pad_maximum_fusion.7), channel_id=1, source_target_pairs={{0,4},{4,8},{8,12},{12,16},{16,20},{20,24},{24,28},{1,5},{5,9},{9,... | collective-permute-start | bytes 1769480 | tf_op jit(solution)/shard_map/ppermute | solution.py:42
  39.9 33.3 %copy-start.24 = (f32[512,768]{0,1:T(8,128)}, f32[512,768]{0,1:T(8,128)S(1)}, u32[]{:S(2)}) copy-start(f32[512,768]{0,1:T(8,128)S(1)} %fusion.161) | copy-start | bytes 4718596
  39.9 29.7 %copy-start.23 = (bf16[512,512]{0,1:T(8,128)(2,1)S(1)}, bf16[512,512]{0,1:T(8,128)(2,1)}, u32[]{:S(2)}) copy-start(bf16[512,512]{0,1:T(8,128)(2,1)} %copy-done.22) | copy-start | bytes 1572868
  39.9 29.7 %copy-start.71 = (bf16[512,1024]{1,0:T(8,128)(2,1)S(1)}, bf16[512,1024]{1,0:T(8,128)(2,1)}, u32[]{:S(2)}) copy-start(bf16[512,1024]{1,0:T(8,128)(2,1)} %param.26) | copy-start | bytes 3145732
  40.0 42.2 %copy-start.28 = (bf16[512,4,32]{0,2,1:T(8,128)(2,1)}, bf16[512,4,32]{0,2,1:T(8,128)(2,1)S(1)}, u32[]{:S(2)}) copy-start(bf16[512,4,32]{0,2,1:T(8,128)(2,1)S(1)} %get-tuple-element.127) | copy-start | bytes 393220
  40.0 42.2 %copy-start.30 = (bf16[512,4,32]{0,2,1:T(8,128)(2,1)}, bf16[512,4,32]{0,2,1:T(8,128)(2,1)S(1)}, u32[]{:S(2)}) copy-start(bf16[512,4,32]{0,2,1:T(8,128)(2,1)S(1)} %get-tuple-element.128) | copy-start | bytes 393220
  73.2 9.0 copy-start.27
  119.5 17.4 %copy-start.49 = (f32[4,512]{1,0:T(4,128)}, f32[4,512]{1,0:T(4,128)S(1)}, u32[]{:S(2)}) copy-start(f32[4,512]{1,0:T(4,128)S(1)} %get-tuple-element.146) | copy-start | bytes 24580
  141.2 95.7 %copy-start.43 = (f32[2048]{0:T(1024)S(1)}, f32[2048]{0:T(1024)}, u32[]{:S(2)}) copy-start(f32[2048]{0:T(1024)} %param.28) | copy-start | bytes 24580
  141.3 509.0 %all-gather.2.cloned.1.call-start = ((), (), s32[]{:S(2)}) async-start(), calls=%async_computation.5 | async-start | bytes 18874368 | tf_op jit(solution)/shard_map/all_gather | solution.py:121
  141.8 762.2 %reduce-scatter.5.cloned.1.call-start = ((), (), s32[]{:S(2)}) async-start(), calls=%async_computation.6 | async-start | bytes 18874368 | tf_op jit(solution)/shard_map/reduce_scatter | solution.py:232
  239.4 4.5 collective-permute-start.4
  251.4 92.9 %collective-permute-start.5 = (bf16[2,512,2048]{2,1,0:T(8,128)(2,1)}, bf16[2,512,2048]{2,1,0:T(8,128)(2,1)}, u32[]{:S(2)}, u32[]{:S(2)}) collective-permute-start(bf16[2,512,2048]{2,1,0:T(8,128)(2,1)} %get-tuple-element.119), channel_id=1, source_target_pairs={{0,8},{4,12},{8,0},{12,4},{16,24},{20,28},{24,16},{28,20},{1,9},{5... | collective-permute-start | bytes 12582920 | tf_op jit(solution)/shard_map/ppermute | solution.py:28
  352.0 15.7 %copy-start.62 = (s32[512,6]{0,1:T(8,128)S(1)}, s32[512,6]{0,1:T(8,128)}, u32[]{:S(2)}) copy-start(s32[512,6]{0,1:T(8,128)} %param.20) | copy-start | bytes 36868
  366.2 189.9 %collective-permute-start.6 = (bf16[4,512,2048]{2,1,0:T(8,128)(2,1)}, bf16[4,512,2048]{2,1,0:T(8,128)(2,1)}, u32[]{:S(2)}, u32[]{:S(2)}) collective-permute-start(bf16[4,512,2048]{2,1,0:T(8,128)(2,1)} %bitcast.238), channel_id=1, source_target_pairs={{0,16},{4,20},{8,24},{12,28},{16,0},{20,4},{24,8},{28,12},{1,17},{... | collective-permute-start | bytes 25165832 | tf_op jit(solution)/shard_map/ppermute | solution.py:28
  569.8 14.1 copy-start.32
  583.9 6.2 copy-start.1
  732.3 40.2 %copy-start.33 = (bf16[2048,64]{0,1:T(8,128)(2,1)S(1)}, bf16[2048,64]{0,1:T(8,128)(2,1)}, u32[]{:S(2)}) copy-start(bf16[2048,64]{0,1:T(8,128)(2,1)} %param.29) | copy-start | bytes 786436
  789.6 208.2 %all-reduce.8.cloned.1.call-start = ((), (), s32[]{:S(2)}) async-start(), calls=%async_computation.8 | async-start | bytes 4194304 | tf_op jit(solution)/shard_map/psum | solution.py:233
  911.2 194.3 %reduce-scatter.7.cloned.1.call-start = ((), (), s32[]{:S(2)}) async-start(), calls=%async_computation.7 | async-start | bytes 18874368 | tf_op jit(solution)/shard_map/reduce_scatter | solution.py:236
  941.1 56.7 %copy-start.44 = (f32[2048]{0:T(1024)S(1)}, f32[2048]{0:T(1024)}, u32[]{:S(2)}) copy-start(f32[2048]{0:T(1024)} %param.28) | copy-start | bytes 24580
  941.1 56.7 %copy-start.46 = (f32[512]{0:T(512)S(1)}, f32[512]{0:T(512)}, u32[]{:S(2)}) copy-start(f32[512]{0:T(512)} %copy-done.45) | copy-start | bytes 6148
  941.1 376.7 %all-reduce.10.cloned.1.call-start = ((), (), s32[]{:S(2)}) async-start(), calls=%async_computation.11 | async-start | bytes 10092544 | tf_op jit(solution)/shard_map/psum | solution.py:290
  951.4 51.3 %copy-start.59 = (f32[512]{0:T(512)S(1)}, f32[512]{0:T(512)}, u32[]{:S(2)}) copy-start(f32[512]{0:T(512)} %copy-done.58) | copy-start | bytes 6148
  997.9 5.0 copy-start.15
  1002.9 5.4 copy-start.50
  1043.2 14.7 copy-start.25
  1075.7 21.0 %collective-permute-start.10 = (bf16[512,576]{0,1:T(8,128)(2,1)}, bf16[512,576]{0,1:T(8,128)(2,1)S(1)}, u32[]{:S(2)}, u32[]{:S(2)}) collective-permute-start(bf16[512,576]{0,1:T(8,128)(2,1)} %get-tuple-element.121), channel_id=1, source_target_pairs={{4,0},{8,4},{12,8},{16,12},{20,16},{24,20},{28,24},{5,1},{9,5},{13... | collective-permute-start | bytes 1769480 | tf_op jit(solution)/shard_map/ppermute | solution.py:42
  1077.0 19.7 %collective-permute-start.7 = (bf16[512,576]{0,1:T(8,128)(2,1)}, bf16[512,576]{0,1:T(8,128)(2,1)S(1)}, u32[]{:S(2)}, u32[]{:S(2)}) collective-permute-start(bf16[512,576]{0,1:T(8,128)(2,1)} %get-tuple-element.120), channel_id=1, source_target_pairs={{16,0},{20,4},{24,8},{28,12},{17,1},{21,5},{25,9},{29,13},{18,2},{... | collective-permute-start | bytes 1769480 | tf_op jit(solution)/shard_map/ppermute | solution.py:42
  1078.3 18.4 %collective-permute-start.8 = (bf16[512,576]{0,1:T(8,128)(2,1)}, bf16[512,576]{0,1:T(8,128)(2,1)}, u32[]{:S(2)}, u32[]{:S(2)}) collective-permute-start(bf16[512,576]{0,1:T(8,128)(2,1)} %get-tuple-element.123), channel_id=1, source_target_pairs={{12,0},{16,4},{20,8},{24,12},{28,16},{13,1},{17,5},{21,9},{25,13},... | collective-permute-start | bytes 1769480 | tf_op jit(solution)/shard_map/ppermute | solution.py:42
  1079.6 5.9 copy-start.38
  1079.6 5.9 copy-start.42
  1079.6 23.4 %collective-permute-start.9 = (bf16[512,576]{0,1:T(8,128)(2,1)S(1)}, bf16[512,576]{0,1:T(8,128)(2,1)}, u32[]{:S(2)}, u32[]{:S(2)}) collective-permute-start(bf16[512,576]{0,1:T(8,128)(2,1)S(1)} %get-tuple-element.122), channel_id=1, source_target_pairs={{8,0},{12,4},{16,8},{20,12},{24,16},{28,20},{9,1},{13,5},{17,9},{2... | collective-permute-start | bytes 1769480 | tf_op jit(solution)/shard_map/ppermute | solution.py:42
  1092.2 10.8 slice-start
  1093.5 9.5 slice-start.1
  1111.4 262.5 %reduce-scatter.11.cloned.1.call-start = ((), (), s32[]{:S(2)}) async-start(), calls=%async_computation.10 | async-start | bytes 9732096 | tf_op jit(solution)/shard_map/reduce_scatter | solution.py:85
  1124.2 323.5 %reduce-scatter.9.cloned.1.call-start = ((), (), s32[]{:S(2)}) async-start(), calls=%async_computation.9 | async-start | bytes 10063872 | tf_op jit(solution)/shard_map/reduce_scatter | solution.py:85
  1131.4 5.2 copy-start.64
  1131.4 5.2 copy-start.66
  1136.6 5.6 copy-start.4
  1136.6 5.6 copy-start.8
  1136.6 5.6 copy-start.16
  1136.7 5.9 copy-start.19
  1136.7 6.3 copy-start.73
  1143.0 176.3 %copy-start.48 = (f32[512]{0:T(512)S(1)}, f32[512]{0:T(512)}, u32[]{:S(2)}) copy-start(f32[512]{0:T(512)} %copy-done.47) | copy-start | bytes 6148
  1143.0 176.3 %copy-start.61 = (f32[512]{0:T(512)S(1)}, f32[512]{0:T(512)}, u32[]{:S(2)}) copy-start(f32[512]{0:T(512)} %param.25) | copy-start | bytes 6148
  1143.0 178.3 %copy-start.57 = (f32[512]{0:T(512)S(1)}, f32[512]{0:T(512)}, u32[]{:S(2)}) copy-start(f32[512]{0:T(512)} %copy-done.56) | copy-start | bytes 6148
  1143.0 178.4 %copy-start.53 = (f32[512]{0:T(512)S(1)}, f32[512]{0:T(512)}, u32[]{:S(2)}) copy-start(f32[512]{0:T(512)} %copy-done.52) | copy-start | bytes 6148
  1143.0 178.4 %copy-start.68 = (f32[32]{0:T(128)S(1)}, f32[32]{0:T(128)}, u32[]{:S(2)}) copy-start(f32[32]{0:T(128)} %copy-done.67) | copy-start | bytes 388
  1321.9 6.7 copy-start.40
  1376.5 21.4 %copy-start.9 = (bf16[8,8,72,352]{3,2,0,1:T(8,128)(2,1)S(1)}, bf16[8,8,72,352]{3,2,0,1:T(8,128)(2,1)}, u32[]{:S(2)}) copy-start(bf16[8,8,72,352]{3,2,0,1:T(8,128)(2,1)} %get-tuple-element.115) | copy-start | bytes 9732100
  1420.2 18.2 %copy-start.55 = (f32[512]{0:T(512)S(1)}, f32[512]{0:T(512)}, u32[]{:S(2)}) copy-start(f32[512]{0:T(512)} %copy-done.54) | copy-start | bytes 6148
  (32 other events, 96.6 us)
Sparse Core Ops, SparseCore 0:
  141.4 91.8 all-reduce.5
  911.4 86.4 all-reduce.7
  1111.5 206.2 all-reduce.9
Sparse Core Ops, SparseCore 1:
  143.8 95.0 all-gather.1
  789.7 114.3 reduce-scatter.4
  941.2 115.7 reduce-scatter.6
  1124.3 95.1 reduce-scatter.10
  1373.9 73.7 reduce-scatter.8
